TPU v7x, 32 devices: a whole 2x2x4 slice. The times are simulated.
32 devices in a mesh: gx: 16 (over z, y, x), gy: 2 (over core).
Axes of the slice: x: 2, y: 2, z: 4, core: 2. Of those that a mesh axis runs over, the one named last changes fastest.
Arguments:
- snapshot: bfloat16 [3, 128, 32, 1024], P(None, 'gx', 'gy'), may hold values from -6 to 6
- basis: bfloat16 [3, 16, 4, 128, 512], P(None, 'gx', 'gy'), may hold values from -3000 to 3000
- taps: bfloat16 [3, 17], replicated, may hold values from 0.099609375 to 1
Outputs:
- new_modes: bfloat16 [3, 16, 4, 128, 512], P(None, 'gx', 'gy')
- new_mode: float32 [3, 16, 4, 128], P(None, 'gx', 'gy')
- factor: float32 [513, 513], replicated
All inputs are finite; a program needn't handle non-finite values.
Results may differ from a plain program's by a relative error of at most 0.0012.
The roundings to bfloat16 on the way count: a program that leaves them out, or rounds other values in their place, can miss the bound.
Values sent between devices are 32-bit elements; how exact they have to be, the bound alone decides.
No kernel may reach another device: no remote copies, remote signals or barrier semaphores. Data moves between devices by JAX's collectives and lax.ppermute only.
A program may use at most 64 MiB of HBM per device.

v0:
```python
import jax
import jax.numpy as jnp
from jax import lax
from jax.sharding import PartitionSpec as P

STRIDE = 8


def padded(block, sides, width, periodic):
    for axis, dim in sides:
        count = lax.axis_size(axis)
        forward = [(i, i + 1) for i in range(count - 1)]
        if periodic:
            forward.append((count - 1, 0))
        backward = [(target, source) for source, target in forward]
        low = lax.ppermute(
            lax.slice_in_dim(block, block.shape[dim] - width, None, axis=dim), axis, forward
        )
        high = lax.ppermute(lax.slice_in_dim(block, 0, width, axis=dim), axis, backward)
        block = jnp.concatenate([low, block, high], axis=dim)
    return block


def band(taps_row, length, out_len, shift, wrap):
    rows = jnp.arange(length, dtype=jnp.int32)[:, None]
    cols = jnp.arange(out_len, dtype=jnp.int32)[None, :]
    lag = rows - STRIDE * cols + shift
    if wrap:
        lag = lag % length
    hits = lag[:, :, None] == jnp.arange(2 * STRIDE + 1, dtype=jnp.int32)[None, None, :]
    return jnp.sum(jnp.where(hits, taps_row[None, None, :], jnp.zeros((), taps_row.dtype)), axis=-1)


def local(snapshot, basis, taps):
    comps, cells_x, cells_y, cells_z = snapshot.shape
    modes = basis.shape[-1]
    flat_rows = basis.reshape(-1, modes)
    total = flat_rows.shape[0] * lax.axis_size("gx") * lax.axis_size("gy")
    mode_part = lax.psum(
        jnp.einsum("rk,rj->kj", flat_rows, flat_rows, preferred_element_type=jnp.float32),
        ("gx", "gy"),
    )
    matrix_z = band(taps[2], cells_z, cells_z // STRIDE, STRIDE, True)
    along_z = jnp.dot(snapshot.reshape(-1, cells_z), matrix_z, preferred_element_type=jnp.float32)
    along_z = along_z.reshape(comps, cells_x, cells_y, cells_z // STRIDE)
    padded_y = padded(along_z, (("gy", 2),), STRIDE, False)
    matrix_y = band(taps[1], cells_y + 2 * STRIDE, cells_y // STRIDE, 0, False).astype(jnp.float32)
    along_y = jnp.einsum("cxyz,yf->cxfz", padded_y, matrix_y, precision=lax.Precision.HIGHEST)
    padded_x = padded(along_y, (("gx", 1),), STRIDE, True)
    matrix_x = band(taps[0], cells_x + 2 * STRIDE, cells_x // STRIDE, 0, False).astype(jnp.float32)
    along_x = jnp.einsum("cxyz,xf->cfyz", padded_x, matrix_x, precision=lax.Precision.HIGHEST)
    filtered = along_x.astype(jnp.bfloat16).reshape(-1)
    stack = jnp.concatenate([flat_rows, filtered[:, None]], axis=1)
    fresh_wide = filtered.astype(jnp.float32)
    cross, square = lax.psum(
        (
            jnp.einsum("rk,r->k", flat_rows, filtered, preferred_element_type=jnp.float32),
            jnp.sum(fresh_wide * fresh_wide),
        ),
        ("gx", "gy"),
    )
    upper_rows = jnp.concatenate([mode_part, cross[:, None]], axis=1)
    last_row = jnp.concatenate([cross, square[None]])[None, :]
    gram = jnp.concatenate([upper_rows, last_row], axis=0)
    gram = gram / total
    lower = jnp.linalg.cholesky(gram)
    solved = lax.linalg.triangular_solve(
        lower, stack.astype(jnp.float32), left_side=False, lower=True, transpose_a=True
    )
    new_modes = solved[:, :modes].astype(jnp.bfloat16).reshape(basis.shape)
    new_mode = solved[:, modes].reshape(basis.shape[:-1])
    return (new_modes, new_mode, lower.T)


def solution(mesh):
    in_specs = (P(None, "gx", "gy", None), P(None, "gx", "gy", None, None), P())
    out_specs = (P(None, "gx", "gy", None, None), P(None, "gx", "gy", None), P())
    return jax.shard_map(local, mesh=mesh, in_specs=in_specs, out_specs=out_specs, check_vma=False)
```

profile of v0, /device:TPU:0, one launch (start us, length us, event | category | flops | bytes accessed | tf_op | source)
XLA Modules:
  0.0 347.1 jit_solution(4015166581742099439)
XLA Ops:
  7.2 0.8 slice_bitcast_fusion.14
  8.3 0.9 fusion.1
  9.2 0.4 convolution_bitcast_fusion.1
  9.8 2.4 collective-permute-start
  12.2 1.3 collective-permute-start.1
  13.5 1.6 convolution_bitcast_fusion
  15.7 2.4 collective-permute-start.2
  18.1 4.1 %collective-permute-start.3 = (f32[3,8,2,128]{3,2,1,0:T(2,128)S(1)}, f32[3,8,2,128]{3,2,1,0:T(2,128)S(1)}, u32[]{:S(2)}, u32[]{:S(2)}) collective-permute-start(f32[3,8,2,128]{3,2,1,0:T(2,128)S(1)} %convolution_bitcast_fusion.2), channel_id=1, source_target_pairs={{2,0},{4,2},{6,4},{8,6},{10,8},{12,10},{14,12},{16,14},{18,16},{20... | collective-permute-start | bytes 73736 | tf_op jit(solution)/shard_map/ppermute | solution.py:19
  22.2 1.7 collective-permute-done.2
  24.1 0.6 multiply_reduce_fusion
  24.9 41.3 %all-reduce.3 = (f32[1]{0:T(128)}, f32[512]{0:T(512)S(1)}) all-reduce(f32[1]{0:T(128)} %bitcast.19, f32[512]{0:T(512)S(1)} %bitcast.151), channel_id=1, replica_groups=mesh['gx'=16,'gy'=2] {'gx','gy'}, use_global_device_ids=true, to_apply=%region_6.7 | all-reduce | flops 513 | bytes 4104 | tf_op jit(solution)/shard_map/psum | solution.py:55
  66.5 0.7 pad_maximum_fusion.4
  67.3 81.6 %all-reduce.6.cloned.1.call-done = f32[512,512]{0,1:T(8,128)} async-done(((f32[512,512]{0,1:T(8,128)}), f32[512,512]{0,1:T(8,128)}) %all-reduce.6.cloned.1.call-update) | async-done | bytes 1048592 | tf_op jit(solution)/shard_map/psum | solution.py:39
  148.9 2.4 maximum_multiply_fusion
  151.3 1.8 copy.62
  153.1 1.5 fusion.10
  154.6 1.0 copy-done.4
  155.6 0.5 cholesky.348
  156.1 11.7 %cholesky.131 = f32[128,128]{1,0:T(8,128)S(1)} custom-call(f32[128,128]{1,0:T(8,128)S(1)} %cholesky.333), custom_call_target="Cholesky" | custom-call | tf_op jit(solution)/shard_map/jit(cholesky)/cholesky | solution.py:66
  168.0 9.8 %custom-call.35 = f32[1,128,128]{1,2,0:T(8,128)S(1)} custom-call(f32[1,128,128]{2,1,0:T(8,128)S(1)} %get-tuple-element.51), custom_call_target="InvertDiagBlocksLowerTriangular" | custom-call | tf_op jit(solution)/shard_map/jit(cholesky)/cholesky | solution.py:66
  177.8 1.4 constant_dynamic-update-slice_fusion.2
  179.2 1.4 convolution_subtract_fusion.3
  180.6 11.7 %cholesky.264 = f32[128,128]{1,0:T(8,128)S(1)} custom-call(f32[128,128]{1,0:T(8,128)S(1)} %cholesky.337), custom_call_target="Cholesky" | custom-call | tf_op jit(solution)/shard_map/jit(cholesky)/cholesky | solution.py:66
  192.4 9.9 %custom-call.36 = f32[1,128,128]{1,2,0:T(8,128)S(1)} custom-call(f32[1,128,128]{2,1,0:T(8,128)S(1)} %get-tuple-element.48), custom_call_target="InvertDiagBlocksLowerTriangular" | custom-call | tf_op jit(solution)/shard_map/jit(cholesky)/cholesky | solution.py:66
  202.3 0.4 convolution_dynamic-update-slice_fusion
  202.7 1.3 convolution_subtract_fusion.4
  204.0 11.7 %cholesky.285 = f32[128,128]{1,0:T(8,128)S(1)} custom-call(f32[128,128]{1,0:T(8,128)S(1)} %cholesky.342), custom_call_target="Cholesky" | custom-call | tf_op jit(solution)/shard_map/jit(cholesky)/cholesky | solution.py:66
  215.8 9.8 %custom-call.37 = f32[1,128,128]{1,2,0:T(8,128)S(1)} custom-call(f32[1,128,128]{2,1,0:T(8,128)S(1)} %get-tuple-element.45), custom_call_target="InvertDiagBlocksLowerTriangular" | custom-call | tf_op jit(solution)/shard_map/jit(cholesky)/cholesky | solution.py:66
  225.8 1.3 convolution_subtract_fusion.5
  227.1 11.9 %cholesky.304 = f32[128,128]{1,0:T(8,128)S(1)} custom-call(f32[128,128]{1,0:T(8,128)S(1)} %cholesky.347), custom_call_target="Cholesky" | custom-call | tf_op jit(solution)/shard_map/jit(cholesky)/cholesky | solution.py:66
  239.1 9.8 %custom-call.38 = f32[1,128,128]{1,2,0:T(8,128)S(1)} custom-call(f32[1,128,128]{2,1,0:T(8,128)S(1)} %get-tuple-element.42), custom_call_target="InvertDiagBlocksLowerTriangular" | custom-call | tf_op jit(solution)/shard_map/jit(cholesky)/cholesky | solution.py:66
  249.2 0.6 multiply_reduce_fusion.1
  251.2 0.7 compare_reduce_fusion.1
  252.0 0.6 compare_reduce_fusion
  252.6 0.6 compare_reduce_fusion.2
  255.8 1.2 fusion.20
  257.0 0.5 triangular_solve.195
  257.6 0.5 copy-done.3
  258.1 11.3 %while.1 = (s32[]{:T(128)}, f32[513,513]{1,0:T(8,128)}, s32[4,2]{0,1:T(2,128)S(1)}, f32[4,128,128]{2,1,0:T(8,128)S(1)}, s32[]{:T(128)}) while((s32[]{:T(128)}, f32[513,513]{1,0:T(8,128)}, s32[4,2]{0,1:T(2,128)S(1)}, f32[4,128,128]{2,1,0:T(8,128)S(1)}, s32[]{:T(128)}) %tuple.51), condition=%wide.while_cond, body=%wide.while_body.sunk | while | flops 2 | bytes 131181 | solution.py:67
  258.2 0.5 fusion.83
  258.7 2.2 bitcast_dynamic-update-slice_fusion.2
  261.0 0.5 fusion.83
  261.5 2.2 bitcast_dynamic-update-slice_fusion.2
  263.8 0.5 fusion.83
  264.4 2.2 bitcast_dynamic-update-slice_fusion.2
  266.7 0.5 fusion.83
  267.2 2.2 bitcast_dynamic-update-slice_fusion.2
  269.4 0.7 fusion.53
  270.2 49.1 %custom-call.39 = f32[5,128,128]{1,2,0:T(8,128)S(1)} custom-call(f32[5,128,128]{2,1,0:T(8,128)S(1)} %pad_maximum_fusion.1), custom_call_target="InvertDiagBlocksLowerTriangular" | custom-call | tf_op jit(solution)/shard_map/triangular_solve | solution.py:67
  319.4 0.6 triangular_solve.205
  319.9 1.1 bitcast_convert_fusion
  321.0 1.6 convolution_subtract_fusion.1
  322.6 0.5 fusion.74
  323.3 2.3 convolution_subtract_fusion.2
  325.6 1.1 fusion.73
  326.9 3.0 convolution_subtract_fusion
  329.9 2.0 fusion.72
  331.9 0.9 copy.73
  332.8 1.9 fusion.17
  334.7 1.0 fusion.34
  335.8 0.6 triangular_solve.193
  336.4 1.1 copy.88
  337.5 1.5 copy.76
  339.0 1.0 pad_maximum_fusion
  (61 shorter events, 3.5 us)
Async XLA Ops:
  7.2 2.1 copy-start
  7.2 141.7 %all-reduce.6.cloned.1.call-start = ((), (), s32[]{:S(2)}) async-start(), calls=%async_computation | async-start | bytes 2097152 | tf_op jit(solution)/shard_map/psum | solution.py:39
  8.3 5.2 %copy-start.1 = (bf16[3,1,2,128,512]{4,3,2,1,0:T(8,128)(2,1)S(1)}, bf16[3,1,2,128,512]{4,3,2,1,0:T(8,128)(2,1)}, u32[]{:S(2)}) copy-start(bf16[3,1,2,128,512]{4,3,2,1,0:T(8,128)(2,1)} %param.4) | copy-start | bytes 2359300
  9.8 5.7 %collective-permute-start = (f32[3,8,8,128]{3,2,1,0:T(8,128)S(1)}, f32[3,8,8,128]{3,2,1,0:T(8,128)S(1)}, u32[]{:S(2)}, u32[]{:S(2)}) collective-permute-start(f32[3,8,8,128]{3,2,1,0:T(8,128)S(1)} %get-tuple-element.39), channel_id=1, source_target_pairs={{0,1},{2,3},{4,5},{6,7},{8,9},{10,11},{12,13},{14,15},{16,17},{18,... | collective-permute-start | bytes 294920 | tf_op jit(solution)/shard_map/ppermute | solution.py:16
  12.2 3.3 collective-permute-start.1
  15.7 8.2 %collective-permute-start.2 = (f32[3,8,2,128]{3,2,1,0:T(2,128)S(1)}, f32[3,8,2,128]{3,2,1,0:T(2,128)S(1)}, u32[]{:S(2)}, u32[]{:S(2)}) collective-permute-start(f32[3,8,2,128]{3,2,1,0:T(2,128)S(1)} %convolution_bitcast_fusion.2), channel_id=1, source_target_pairs={{0,2},{2,4},{4,6},{6,8},{8,10},{10,12},{12,14},{14,16},{16,18},{18... | collective-permute-start | bytes 73736 | tf_op jit(solution)/shard_map/ppermute | solution.py:16
  18.1 5.8 %collective-permute-start.3 = (f32[3,8,2,128]{3,2,1,0:T(2,128)S(1)}, f32[3,8,2,128]{3,2,1,0:T(2,128)S(1)}, u32[]{:S(2)}, u32[]{:S(2)}) collective-permute-start(f32[3,8,2,128]{3,2,1,0:T(2,128)S(1)} %convolution_bitcast_fusion.2), channel_id=1, source_target_pairs={{2,0},{4,2},{6,4},{8,6},{10,8},{12,10},{14,12},{16,14},{18,16},{20... | collective-permute-start | bytes 73736 | tf_op jit(solution)/shard_map/ppermute | solution.py:19
  154.5 1.1 copy-start.4
  255.8 2.3 copy-start.7
  257.0 1.1 copy-start.3
  319.4 6.2 %copy-start.8 = (f32[5,128,128]{1,2,0:T(8,128)}, f32[5,128,128]{1,2,0:T(8,128)S(1)}, u32[]{:S(2)}) copy-start(f32[5,128,128]{1,2,0:T(8,128)S(1)} %custom-call.39) | copy-start | bytes 983044
  334.7 2.7 copy-start.2
  337.5 1.6 copy-start.5
  337.5 1.6 copy-start.6
Sparse Core Ops, SparseCore 0:
  15.2 133.6 all-reduce.5
where the time goes:
time: 351 us; the launch traced here: 347 us
  other arithmetic  149 us (42%)
  waiting for transfers between devices  83.3 us (24%)
  blocking collectives  41.3 us (12%)
  local copies, waits for them, and re-layouts  22.5 us (6%)
  matrix products  22.2 us (6%)
  between operations  18.6 us (5%)
  starting transfers between devices  10.2 us (3%)
    another operation x16, other arithmetic, local(): lower = jnp.linalg.cholesky(gram)  89.1 us
    psum x1, waiting for transfers between devices, local(): lax.psum(jnp.einsum('rk,rj->kj', flat_rows, flat_rows, preferred_element_...  81.6 us
    another operation x8, other arithmetic, local(): lax.linalg.triangular_solve(lower, stack.astype(jnp.float32), left_side=F...  52 us
    psum x1, blocking collectives, local(): lax.psum((jnp.einsum('rk,r->k', flat_rows, filtered, preferred_element_ty...  41.3 us
    another operation x8, matrix products, local(): lax.linalg.triangular_solve(lower, stack.astype(jnp.float32), left_side=F...  13.5 us
    another operation x12, local copies, waits for them, and re-layouts  11.3 us
  transfers between devices with their start and end apart: 5, of which 2 were waited for; matrix products, arithmetic and copies ran while one was open for 1% of the time, Pallas kernels for 0%

commit v1 on v0

--- a/solution.py
+++ b/solution.py
@@ -1,9 +1,17 @@
+import functools
 import jax
 import jax.numpy as jnp
 from jax import lax
 from jax.sharding import PartitionSpec as P
 
 STRIDE = 8
+
+
+def write_gates(original, device_axis):
+    return jax.lax.all_gather(original, axis_name=device_axis).sum(axis=0)
+
+
+read_numbers_now = functools.partial(write_gates, device_axis=("gx", "gy"))
 
 
 def padded(block, sides, width, periodic):
@@ -36,9 +44,8 @@
     modes = basis.shape[-1]
     flat_rows = basis.reshape(-1, modes)
     total = flat_rows.shape[0] * lax.axis_size("gx") * lax.axis_size("gy")
-    mode_part = lax.psum(
-        jnp.einsum("rk,rj->kj", flat_rows, flat_rows, preferred_element_type=jnp.float32),
-        ("gx", "gy"),
+    mode_part = read_numbers_now(
+        jnp.einsum("rk,rj->kj", flat_rows, flat_rows, preferred_element_type=jnp.float32)
     )
     matrix_z = band(taps[2], cells_z, cells_z // STRIDE, STRIDE, True)
     along_z = jnp.dot(snapshot.reshape(-1, cells_z), matrix_z, preferred_element_type=jnp.float32)

time: 351 us -> 432 us (1.23)
  waiting for transfers between devices: 83.3 us -> 142 us
  other arithmetic: 149 us -> 162 us
  local copies, waits for them, and re-layouts: 22.5 us -> 27.9 us
    all_gather x0 -> x1, waiting for transfers between devices: none -> 138 us  [write_gates(): return jax.lax.all_gather(original, axis_name=device_axis).sum(axis=0)]
    psum x1 -> x0, waiting for transfers between devices: 81.6 us -> none  [local(): lax.psum(jnp.einsum('rk,rj->kj', flat_rows, flat_rows, preferred_element_...]
    reduce_sum x0 -> x1, other arithmetic: none -> 13.7 us  [write_gates(): return jax.lax.all_gather(original, axis_name=device_axis).sum(axis=0)]
  transfers between devices with their start and end apart: 5 -> 5, of which waited for: 2 -> 4; matrix products, arithmetic and copies ran while one was open for 1% -> 1% of each run, Pallas kernels for 0% -> 0%
where the time goes in v1:
time: 432 us; the launch traced here: 427 us
  other arithmetic  162 us (38%)
  waiting for transfers between devices  142 us (33%)
  blocking collectives  42.9 us (10%)
  local copies, waits for them, and re-layouts  27.9 us (6%)
  matrix products  23.6 us (5%)
  between operations  18.6 us (4%)
  starting transfers between devices  10.2 us (2%)
    all_gather x1, waiting for transfers between devices, write_gates(): return jax.lax.all_gather(original, axis_name=device_axis).sum(axis=0)  138 us
    another operation x16, other arithmetic, local(): lower = jnp.linalg.cholesky(gram)  89.1 us
    another operation x8, other arithmetic, local(): lax.linalg.triangular_solve(lower, stack.astype(jnp.float32), left_side=F...  52.9 us
    psum x1, blocking collectives, local(): lax.psum((jnp.einsum('rk,r->k', flat_rows, filtered, preferred_element_ty...  42.9 us
    another operation x12, local copies, waits for them, and re-layouts  14.2 us
    reduce_sum x1, other arithmetic, write_gates(): return jax.lax.all_gather(original, axis_name=device_axis).sum(axis=0)  13.7 us
    another operation x8, matrix products, local(): lax.linalg.triangular_solve(lower, stack.astype(jnp.float32), left_side=F...  13.5 us
  transfers between devices with their start and end apart: 5, of which 4 were waited for; matrix products, arithmetic and copies ran while one was open for 1% of the time, Pallas kernels for 0%

profile of v1, /device:TPU:0, one launch (start us, length us, event | category | flops | bytes accessed | tf_op | source)
XLA Modules:
  0.0 427.2 jit_solution(13529952083618031544)
XLA Ops:
  7.2 3.0 convolution_bitcast_fusion
  10.5 0.9 fusion.1
  12.0 2.4 collective-permute-start
  14.5 1.3 collective-permute-start.1
  16.1 1.5 collective-permute-done.1
  17.9 2.4 collective-permute-start.2
  20.3 4.1 collective-permute-start.3
  24.3 1.7 collective-permute-done.2
  26.3 0.6 multiply_reduce_fusion
  27.2 42.9 %all-reduce.3 = (f32[1]{0:T(128)}, f32[512]{0:T(512)S(1)}) all-reduce(f32[1]{0:T(128)} %bitcast.21, f32[512]{0:T(512)S(1)} %bitcast.155), channel_id=1, replica_groups=mesh['gx'=16,'gy'=2] {'gx','gy'}, use_global_device_ids=true, to_apply=%region_6.7 | all-reduce | flops 513 | bytes 4104 | tf_op jit(solution)/shard_map/psum | solution.py:62
  70.4 0.7 pad_maximum_fusion.4
  71.2 138.2 %all-gather.3.cloned.1.call-done = f32[16384,512]{1,0:T(8,128)} async-done(((f32[512,512]{1,0:T(8,128)}), f32[16384,512]{1,0:T(8,128)}) %all-gather.3.cloned.1.call-update) | async-done | bytes 33554448 | tf_op jit(solution)/shard_map/all_gather | solution.py:11
  209.4 13.7 %reduce_sum.54 = f32[512,512]{1,0:T(8,128)} reduce(f32[32,512,512]{2,1,0:T(8,128)} %bitcast.136, f32[]{:T(128)} %constant.182.clone.1), dimensions={0}, to_apply=%region_0.0 | reduce | flops 8126464 | bytes 34603012 | tf_op jit(solution)/shard_map/reduce_sum | solution.py:11
  223.1 1.6 copy.77
  224.7 1.2 maximum_multiply_fusion
  225.9 2.9 copy.79
  228.7 1.5 fusion.10
  230.3 1.1 copy-done.4
  231.3 11.7 %cholesky.131 = f32[128,128]{1,0:T(8,128)S(1)} custom-call(f32[128,128]{1,0:T(8,128)S(1)} %cholesky.333), custom_call_target="Cholesky" | custom-call | tf_op jit(solution)/shard_map/jit(cholesky)/cholesky | solution.py:73
  243.2 1.2 cholesky.348
  244.4 9.8 %custom-call.35 = f32[1,128,128]{1,2,0:T(8,128)S(1)} custom-call(f32[1,128,128]{2,1,0:T(8,128)S(1)} %get-tuple-element.54), custom_call_target="InvertDiagBlocksLowerTriangular" | custom-call | tf_op jit(solution)/shard_map/jit(cholesky)/cholesky | solution.py:73
  254.2 1.4 constant_dynamic-update-slice_fusion.2
  255.6 1.4 convolution_subtract_fusion.3
  257.0 11.7 %cholesky.264 = f32[128,128]{1,0:T(8,128)S(1)} custom-call(f32[128,128]{1,0:T(8,128)S(1)} %cholesky.337), custom_call_target="Cholesky" | custom-call | tf_op jit(solution)/shard_map/jit(cholesky)/cholesky | solution.py:73
  268.8 9.9 %custom-call.36 = f32[1,128,128]{1,2,0:T(8,128)S(1)} custom-call(f32[1,128,128]{2,1,0:T(8,128)S(1)} %get-tuple-element.51), custom_call_target="InvertDiagBlocksLowerTriangular" | custom-call | tf_op jit(solution)/shard_map/jit(cholesky)/cholesky | solution.py:73
  279.1 1.3 convolution_subtract_fusion.4
  280.4 11.7 %cholesky.285 = f32[128,128]{1,0:T(8,128)S(1)} custom-call(f32[128,128]{1,0:T(8,128)S(1)} %cholesky.342), custom_call_target="Cholesky" | custom-call | tf_op jit(solution)/shard_map/jit(cholesky)/cholesky | solution.py:73
  292.1 9.8 %custom-call.37 = f32[1,128,128]{1,2,0:T(8,128)S(1)} custom-call(f32[1,128,128]{2,1,0:T(8,128)S(1)} %get-tuple-element.48), custom_call_target="InvertDiagBlocksLowerTriangular" | custom-call | tf_op jit(solution)/shard_map/jit(cholesky)/cholesky | solution.py:73
  302.2 1.3 convolution_subtract_fusion.5
  303.5 11.9 %cholesky.304 = f32[128,128]{1,0:T(8,128)S(1)} custom-call(f32[128,128]{1,0:T(8,128)S(1)} %cholesky.347), custom_call_target="Cholesky" | custom-call | tf_op jit(solution)/shard_map/jit(cholesky)/cholesky | solution.py:73
  315.5 9.8 %custom-call.38 = f32[1,128,128]{1,2,0:T(8,128)S(1)} custom-call(f32[1,128,128]{2,1,0:T(8,128)S(1)} %get-tuple-element.45), custom_call_target="InvertDiagBlocksLowerTriangular" | custom-call | tf_op jit(solution)/shard_map/jit(cholesky)/cholesky | solution.py:73
  325.6 0.6 multiply_reduce_fusion.1
  327.6 0.7 compare_reduce_fusion.1
  328.3 0.6 compare_reduce_fusion
  329.0 0.6 compare_reduce_fusion.2
  332.1 1.2 fusion.20
  333.4 0.5 triangular_solve.195
  333.9 0.5 copy-done.3
  334.5 14.2 %while.1 = (s32[]{:T(128)}, f32[513,513]{1,0:T(8,128)}, s32[4,2]{0,1:T(2,128)S(1)}, f32[4,128,128]{2,1,0:T(8,128)}, s32[]{:T(128)}) while((s32[]{:T(128)}, f32[513,513]{1,0:T(8,128)}, s32[4,2]{0,1:T(2,128)S(1)}, f32[4,128,128]{2,1,0:T(8,128)}, s32[]{:T(128)}) %tuple.51), condition=%wide.while_cond, body=%wide.while_body.sunk | while | flops 2 | bytes 132705 | solution.py:74
  334.5 0.6 fusion.83
  335.1 2.9 bitcast_dynamic-update-slice_fusion.2
  338.1 0.6 fusion.83
  338.7 2.9 bitcast_dynamic-update-slice_fusion.2
  341.6 0.6 fusion.83
  342.2 2.9 bitcast_dynamic-update-slice_fusion.2
  345.2 0.6 fusion.83
  345.8 2.9 bitcast_dynamic-update-slice_fusion.2
  348.6 0.7 fusion.53
  349.4 1.0 pad_maximum_fusion.1
  350.3 49.1 %custom-call.39 = f32[5,128,128]{1,2,0:T(8,128)S(1)} custom-call(f32[5,128,128]{2,1,0:T(8,128)S(1)} %pad_maximum_fusion.1), custom_call_target="InvertDiagBlocksLowerTriangular" | custom-call | tf_op jit(solution)/shard_map/triangular_solve | solution.py:74
  399.5 0.6 triangular_solve.205
  400.1 1.1 bitcast_convert_fusion
  401.1 1.6 convolution_subtract_fusion.1
  403.4 2.3 convolution_subtract_fusion.2
  405.7 1.1 fusion.73
  407.0 3.0 convolution_subtract_fusion
  410.0 2.0 fusion.72
  412.0 0.9 copy.90
  412.9 1.9 fusion.17
  414.9 1.0 fusion.34
  415.9 0.6 triangular_solve.193
  416.5 1.1 copy.104
  417.6 1.5 copy.93
  419.2 1.0 pad_maximum_fusion
  (63 shorter events, 4.7 us)
Async XLA Ops:
  7.2 4.3 %copy-start = (bf16[3,8,16,1024]{3,2,1,0:T(8,128)(2,1)S(1)}, bf16[3,8,16,1024]{3,2,1,0:T(8,128)(2,1)}, u32[]{:S(2)}) copy-start(bf16[3,8,16,1024]{3,2,1,0:T(8,128)(2,1)} %param.3) | copy-start | bytes 2359300
  7.2 3.1 copy-start.8
  7.2 202.2 %all-gather.3.cloned.1.call-start = ((), (), s32[]{:S(2)}) async-start(), calls=%async_computation | async-start | bytes 34603008 | tf_op jit(solution)/shard_map/all_gather | solution.py:11
  11.5 15.5 %copy-start.1 = (bf16[3,1,2,128,512]{4,3,2,1,0:T(8,128)(2,1)S(1)}, bf16[3,1,2,128,512]{4,3,2,1,0:T(8,128)(2,1)}, u32[]{:S(2)}) copy-start(bf16[3,1,2,128,512]{4,3,2,1,0:T(8,128)(2,1)} %param.4) | copy-start | bytes 2359300
  12.0 4.1 collective-permute-start
  14.5 3.2 collective-permute-start.1
  17.9 8.2 %collective-permute-start.2 = (f32[3,8,2,128]{3,2,1,0:T(2,128)S(1)}, f32[3,8,2,128]{3,2,1,0:T(2,128)S(1)}, u32[]{:S(2)}, u32[]{:S(2)}) collective-permute-start(f32[3,8,2,128]{3,2,1,0:T(2,128)S(1)} %convolution_bitcast_fusion.2), channel_id=1, source_target_pairs={{0,2},{2,4},{4,6},{6,8},{8,10},{10,12},{12,14},{14,16},{16,18},{18... | collective-permute-start | bytes 73736 | tf_op jit(solution)/shard_map/ppermute | solution.py:24
  20.3 5.9 %collective-permute-start.3 = (f32[3,8,2,128]{3,2,1,0:T(2,128)S(1)}, f32[3,8,2,128]{3,2,1,0:T(2,128)S(1)}, u32[]{:S(2)}, u32[]{:S(2)}) collective-permute-start(f32[3,8,2,128]{3,2,1,0:T(2,128)S(1)} %convolution_bitcast_fusion.2), channel_id=1, source_target_pairs={{2,0},{4,2},{6,4},{8,6},{10,8},{12,10},{14,12},{16,14},{18,16},{20... | collective-permute-start | bytes 73736 | tf_op jit(solution)/shard_map/ppermute | solution.py:27
  230.3 1.1 copy-start.4
  333.4 1.1 copy-start.3
  399.5 6.2 %copy-start.7 = (f32[5,128,128]{1,2,0:T(8,128)}, f32[5,128,128]{1,2,0:T(8,128)S(1)}, u32[]{:S(2)}) copy-start(f32[5,128,128]{1,2,0:T(8,128)S(1)} %custom-call.39) | copy-start | bytes 983044
  414.9 2.7 copy-start.2
  417.6 1.6 copy-start.5
  417.6 1.6 copy-start.6
Sparse Core Ops, SparseCore 0:
  11.4 197.9 all-gather.2
